TPU v7x, 32 devices: a whole 2x2x4 slice. The times are simulated.
32 devices in a mesh: gx: 8 (over z, x), gy: 4 (over y, core).
Axes of the slice: x: 2, y: 2, z: 4, core: 2. Of those that a mesh axis runs over, the one named last changes fastest.
Arguments:
- right_side: float32 [128, 128, 128], P('gx', 'gy'), may hold values from -13 to 13
- accumulation: float32 [128, 128, 128], P('gx', 'gy'), may hold values from 0.05 to 0.5
- trans_x: float32 [128, 128, 128], P('gx', 'gy'), may hold values from 0.1 to 2
- trans_y: float32 [128, 128, 128], P('gx', 'gy'), may hold values from 0.1 to 2
- trans_z: float32 [128, 128, 128], P('gx', 'gy'), may hold values from 0.1 to 2
- perf_cells: int32 [512, 256], P(('gx', 'gy')), may hold values from 0 to 65535
- perf_live: int32 [512, 256], P(('gx', 'gy')), may hold values 0 or 1
- well_region: int32 [512, 1], P(('gx', 'gy')), may hold values from 0 to 7; in each aligned block of 16 rows (0 to 15, 16 to 31, ...) at most 2 rows name the same one
- schur_blocks: float32 [512, 256, 256], P(('gx', 'gy')), may hold values from -8 to 10, as said below
Outputs:
- pressure_update: float32 [128, 128, 128], P('gx', 'gy')
- residual: float32 [128, 128, 128], P('gx', 'gy')
Inputs may be any that keep to these rules, and one draw needn't show every extreme that they name: `perf_cells`: well w is owned by the device at position w // 16 of gx+gy; its slot's cell is a flat index (x slowest, layer fastest) within the block of 16 x 32 x 128 cells of the device at x index well_region[w] and at the owner's y index. `well_region`: among the wells of one owner, no x index is named more than 2 times, and some x index exactly 2 times. `schur_blocks`: each block is symmetric positive definite.
All inputs are finite; a program needn't handle non-finite values. No bound on the sum of `perf_live` on one device may be relied on, other than what follows from the above.
Results may differ from a plain program's by a relative error of at most 0.0003.
Values sent between devices are 32-bit elements; how exact they have to be, the bound alone decides.
A program may use at most 64 MiB of HBM per device.

v0:
```python
import jax
import jax.numpy as jnp
from jax import lax
from jax.sharding import PartitionSpec as P

WCAP = 2
ITERS = 6


def from_behind(value, axis, steps):
    count = lax.axis_size(axis)
    leading, last = (max(0, -steps), min(count, count - steps))
    return lax.ppermute(value, axis, [(source, source + steps) for source in range(leading, last)])


def with_halo(x, sides, width):
    for axis, dim in sides:
        size, length = (lax.axis_size(axis), x.shape[dim])
        up = [(i, (i + 1) % size) for i in range(size - 1)]
        down = [(j, i) for i, j in up]
        last = lax.slice_in_dim(x, length - width, length, axis=dim)
        leading = lax.slice_in_dim(x, 0, width, axis=dim)
        before = lax.ppermute(last, axis, up)
        after = lax.ppermute(leading, axis, down)
        x = jnp.concatenate([before, x, after], axis=dim)
    return x


def shifted_layer(values, upward):
    zeros_layer = jnp.zeros_like(values[:, :, :1])
    if upward:
        return jnp.concatenate([values[:, :, 1:], zeros_layer], 2)
    return jnp.concatenate([zeros_layer, values[:, :, :-1]], 2)


def column_table(col_ids, columns):
    return (col_ids[:, None] == jnp.arange(columns, dtype=jnp.int32)[None, :]).astype(jnp.float32)


def layer_table(lay_ids, layers):
    return (lay_ids[:, None] == jnp.arange(layers, dtype=jnp.int32)[None, :]).astype(jnp.float32)


def pick_cells(field, col_ids, lay_ids):
    columns = field.shape[0] * field.shape[1]
    layers = field.shape[2]
    field_cols = field.reshape(columns, layers)

    def pick_block(pair):
        rows_sel = jnp.dot(
            column_table(pair[0], columns), field_cols, precision=lax.Precision.HIGHEST
        )
        return jnp.sum(rows_sel * layer_table(pair[1], layers), axis=1)

    return lax.map(pick_block, (col_ids, lay_ids))


def add_cells(values, col_ids, lay_ids, shape):
    columns = shape[0] * shape[1]
    layers = shape[2]

    def add_block(total, triple):
        spread_rows = layer_table(triple[1], layers) * triple[2][:, None]
        added = lax.dot_general(
            column_table(triple[0], columns),
            spread_rows,
            (((0,), (0,)), ((), ())),
            precision=lax.Precision.HIGHEST,
        )
        return (total + added, None)

    start = jnp.zeros((columns, layers), jnp.float32)
    total, unused = lax.scan(add_block, start, (col_ids, lay_ids, values))
    return total.reshape(shape)


def local(
    right_side,
    accumulation,
    trans_x,
    trans_y,
    trans_z,
    perf_cells,
    perf_live,
    well_region,
    schur_blocks,
):
    rows_x, rows_y, layers = right_side.shape
    width_x = lax.axis_size("gx")
    last_x = lax.axis_index("gx") == width_x - 1
    last_y = lax.axis_index("gy") == lax.axis_size("gy") - 1
    face_x = trans_x.at[-1].set(jnp.where(last_x, 0.0, trans_x[-1]))
    face_y = trans_y.at[:, -1].set(jnp.where(last_y, 0.0, trans_y[:, -1]))
    face_z = trans_z.at[:, :, -1].set(0.0)
    below_x = from_behind(face_x[-1:], "gx", 1)
    below_y = from_behind(face_y[:, -1:], "gy", 1)
    prev_x = jnp.concatenate([below_x, face_x[:-1]], 0)
    prev_y = jnp.concatenate([below_y, face_y[:, :-1]], 1)
    prev_z = shifted_layer(face_z, False)
    diagonal = accumulation + face_x + prev_x + face_y + prev_y + face_z + prev_z
    region = well_region[:, 0]
    wells_here = region.shape[0]
    perforations = perf_cells.shape[1]
    numbered = jnp.arange(wells_here, dtype=jnp.int32)
    earlier = (region[:, None] == region[None, :]) & (numbered[None, :] < numbered[:, None])
    ranking = jnp.sum(earlier.astype(jnp.int32), axis=1)
    slot_index = region * WCAP + ranking
    slots_total = width_x * WCAP
    live_mask = perf_live.astype(jnp.float32)
    requests = jnp.zeros((slots_total, perforations), jnp.int32).at[slot_index].set(perf_cells)
    requests = requests.reshape(width_x, WCAP, perforations)
    wanted = lax.all_to_all(requests, "gx", split_axis=0, concat_axis=0, tiled=True).reshape(
        width_x, WCAP * perforations
    )
    col_ids = wanted // layers
    lay_ids = wanted % layers
    field_shape = (rows_x, rows_y, layers)
    slot_table = (slot_index[:, None] == jnp.arange(slots_total, dtype=jnp.int32)[None, :]).astype(
        jnp.float32
    )

    def well_term(field):
        picked = pick_cells(field, col_ids, lay_ids).reshape(width_x, WCAP, perforations)
        arrived = lax.all_to_all(picked, "gx", split_axis=0, concat_axis=0, tiled=True).reshape(
            slots_total, perforations
        )
        gathered = jnp.dot(slot_table, arrived, precision=lax.Precision.HIGHEST) * live_mask
        pushed = (
            jnp.einsum("wij,wj->wi", schur_blocks, gathered, precision=lax.Precision.HIGHEST)
            * live_mask
        )
        outgoing = lax.dot_general(
            slot_table, pushed, (((0,), (0,)), ((), ())), precision=lax.Precision.HIGHEST
        )
        outgoing = outgoing.reshape(width_x, WCAP, perforations)
        returned = lax.all_to_all(outgoing, "gx", split_axis=0, concat_axis=0, tiled=True)
        return add_cells(
            returned.reshape(width_x, WCAP * perforations), col_ids, lay_ids, field_shape
        )

    def operate(field):
        padded = with_halo(field, (("gx", 0), ("gy", 1)), 1)
        local_part = (
            accumulation * field
            + face_x * (field - padded[2:, 1:-1])
            + prev_x * (field - padded[:-2, 1:-1])
            + face_y * (field - padded[1:-1, 2:])
            + prev_y * (field - padded[1:-1, :-2])
            + face_z * (field - shifted_layer(field, True))
            + prev_z * (field - shifted_layer(field, False))
        )
        return local_part + well_term(field)

    solution = jnp.zeros_like(right_side)
    residual = right_side

    def paired(residual):
        precon = residual / diagonal
        applied = operate(precon)
        sums_pair = lax.psum((jnp.sum(residual * precon), jnp.sum(precon * applied)), ("gx", "gy"))
        return (precon, applied, sums_pair[0], sums_pair[1])

    precon, applied, product_now, curvature = paired(residual)
    step_size = product_now / curvature

    def iterate(counter, carried):
        solution, residual, direction, conjugate, step_size, product_now = carried
        solution = solution + step_size * direction
        residual = residual - step_size * conjugate
        precon, applied, product_next, curvature = paired(residual)
        ratio = product_next / product_now
        step_next = product_next / (curvature - ratio * product_next / step_size)
        direction = precon + ratio * direction
        conjugate = applied + ratio * conjugate
        return (solution, residual, direction, conjugate, step_next, product_next)

    solution, residual, direction, conjugate, step_size, product_now = lax.fori_loop(
        0, ITERS - 1, iterate, (solution, residual, precon, applied, step_size, product_now)
    )
    solution = solution + step_size * direction
    residual = residual - step_size * conjugate
    return (solution, residual)


def solution(mesh):
    placed = (
        P("gx", "gy", None),
        P("gx", "gy", None),
        P("gx", "gy", None),
        P("gx", "gy", None),
        P("gx", "gy", None),
        P(("gx", "gy"), None),
        P(("gx", "gy"), None),
        P(("gx", "gy"), None),
        P(("gx", "gy"), None, None),
    )
    return jax.shard_map(
        local,
        mesh=mesh,
        in_specs=placed,
        out_specs=(P("gx", "gy", None), P("gx", "gy", None)),
        check_vma=False,
    )
```

profile of v0, /device:TPU:0, one launch (start us, length us, event | category | flops | bytes accessed | tf_op | source)
XLA Modules:
  0.0 626.5 jit_solution(16495246734322726971)
XLA Ops:
  4.4 4.9 collective-permute-start.4
  17.2 2.0 fusion.75
  19.2 4.9 all-to-all-start.2
  24.2 6.4 %all-to-all-done.2 = s32[8,2,256]{2,1,0:T(2,128)S(1)} async-done(((s32[8,2,256]{2,1,0:T(2,128)}), s32[8,2,256]{2,1,0:T(2,128)S(1)}, u32[]{:S(2)}, u32[]{:S(2)}) %all-to-all-start.2) | async-done | bytes 16416 | tf_op jit(solution)/shard_map/all_to_all | solution.py:112
  30.6 7.2 %while.68 = (s32[]{:T(128)}, f32[8,512]{1,0:T(8,128)S(1)}, s32[8,512]{1,0:T(8,128)S(1)}, s32[8,512]{1,0:T(8,128)S(1)}, f32[512,128]{1,0:T(8,128)S(1)}, /*index=5*/s32[]{:T(128)}, s32[]{:T(128)}) while((s32[]{:T(128)}, f32[8,512]{1,0:T(8,128)S(1)}, s32[8,512]{1,0:T(8,128)S(1)}, s32[8,512]{1,0:T(8,128)S(1)}, f32[512,128]{1,0:T(8,128)S(1)}, ...), condition=%wide.region_4.5_spmd, body=%wide.region_2.4_spmd.sunk | while | flops 403111424 | bytes 280661 | solution.py:55
  38.5 3.3 all-to-all-start.3
  43.1 4.5 collective-permute-start.7
  49.1 5.7 fusion.60
  56.3 5.3 all-to-all-start.4
  62.9 3.0 collective-permute-start.9
  66.0 2.2 all-to-all-done.4
  68.2 10.5 %while.69 = (s32[]{:T(128)}, f32[512,128]{1,0:T(8,128)S(1)}, s32[8,512]{1,0:T(8,128)S(1)}, s32[8,512]{1,0:T(8,128)S(1)}, f32[8,512]{1,0:T(8,128)S(1)}, /*index=5*/s32[]{:T(128)}, s32[]{:T(128)}) while((s32[]{:T(128)}, f32[512,128]{1,0:T(8,128)S(1)}, s32[8,512]{1,0:T(8,128)S(1)}, s32[8,512]{1,0:T(8,128)S(1)}, ...), condition=%wide.region_6.7_spmd.clone, body=%wide.region_5.6_spmd.clone.sunk | while | flops 403177472 | bytes 542815 | solution.py:73
  79.8 39.4 %all-reduce.6 = (f32[]{:T(128)}, f32[]{:T(128)}) all-reduce(f32[]{:T(128)} %get-tuple-element.372, f32[]{:T(128)} %get-tuple-element.371), channel_id=1, replica_groups=mesh['gx'=8,'gy'=4] {'gx','gy'}, use_global_device_ids=true, to_apply=%region_8.9 | all-reduce | flops 2 | bytes 16 | tf_op jit(solution)/shard_map/psum | solution.py:160
  120.5 505.1 %while.72 = (s32[]{:T(128)}, f32[16,32,128]{2,1,0:T(8,128)S(1)}, f32[16,32,128]{2,1,0:T(8,128)S(1)}, f32[16,32,128]{2,1,0:T(8,128)S(1)}, f32[16,32,128]{2,1,0:T(...) while((s32[]{:T(128)}, f32[16,32,128]{2,1,0:T(8,128)S(1)}, ...), condition=%wide.region_21.22_spmd.clone, body=%wide.region_11.0_spmd.clone.sunk | while | flops 823215616 | bytes 14914575 | solution.py:177
  123.0 4.8 collective-permute-start.1
  127.8 7.1 %while.73 = (s32[]{:T(128)}, f32[8,512]{1,0:T(8,128)S(1)}, s32[8,512]{1,0:T(8,128)S(1)}, s32[8,512]{1,0:T(8,128)S(1)}, f32[512,128]{1,0:T(8,128)S(1)}, /*index=5*/s32[]{:T(128)}, s32[]{:T(128)}) while((s32[]{:T(128)}, f32[8,512]{1,0:T(8,128)S(1)}, s32[8,512]{1,0:T(8,128)S(1)}, s32[8,512]{1,0:T(8,128)S(1)}, f32[512,128]{1,0:T(8,128)S(1)}, ...), condition=%wide.region_16.16_spmd, body=%wide.region_14.15_spmd.sunk | while | flops 403111424 | bytes 280661 | solution.py:55
  135.6 6.0 all-to-all-start
  142.3 5.9 all-to-all-done
  149.1 5.7 fusion.112
  156.4 3.3 all-to-all-start.1
  162.4 3.9 all-to-all-done.1
  166.2 10.5 %while.74 = (s32[]{:T(128)}, f32[512,128]{1,0:T(8,128)S(1)}, s32[8,512]{1,0:T(8,128)S(1)}, s32[8,512]{1,0:T(8,128)S(1)}, f32[8,512]{1,0:T(8,128)S(1)}, /*index=5*/s32[]{:T(128)}, s32[]{:T(128)}) while((s32[]{:T(128)}, f32[512,128]{1,0:T(8,128)S(1)}, s32[8,512]{1,0:T(8,128)S(1)}, s32[8,512]{1,0:T(8,128)S(1)}, ...), condition=%wide.region_18.18_spmd.clone, body=%wide.region_17.17_spmd.clone.sunk | while | flops 403177472 | bytes 542815 | solution.py:73
  177.5 2.1 multiply_reduce_fusion.5
  179.6 39.3 %all-reduce.8 = (f32[]{:T(128)}, f32[]{:T(128)}) all-reduce(f32[]{:T(128)} %get-tuple-element.792, f32[]{:T(128)} %get-tuple-element.793), channel_id=1, replica_groups=mesh['gx'=8,'gy'=4] {'gx','gy'}, use_global_device_ids=true, to_apply=%region_13.13 | all-reduce | flops 2 | bytes 16 | tf_op jit(solution)/shard_map/while/body/eval_jaxpr/psum | solution.py:160
  224.0 4.8 collective-permute-start.1
  228.8 7.2 %while.73 = (s32[]{:T(128)}, f32[8,512]{1,0:T(8,128)S(1)}, s32[8,512]{1,0:T(8,128)S(1)}, s32[8,512]{1,0:T(8,128)S(1)}, f32[512,128]{1,0:T(8,128)S(1)}, /*index=5*/s32[]{:T(128)}, s32[]{:T(128)}) while((s32[]{:T(128)}, f32[8,512]{1,0:T(8,128)S(1)}, s32[8,512]{1,0:T(8,128)S(1)}, s32[8,512]{1,0:T(8,128)S(1)}, f32[512,128]{1,0:T(8,128)S(1)}, ...), condition=%wide.region_16.16_spmd, body=%wide.region_14.15_spmd.sunk | while | flops 403111424 | bytes 280661 | solution.py:55
  236.7 6.0 all-to-all-start
  243.4 5.9 all-to-all-done
  250.2 5.7 fusion.112
  257.4 3.3 all-to-all-start.1
  263.4 3.9 all-to-all-done.1
  267.3 10.5 %while.74 = (s32[]{:T(128)}, f32[512,128]{1,0:T(8,128)S(1)}, s32[8,512]{1,0:T(8,128)S(1)}, s32[8,512]{1,0:T(8,128)S(1)}, f32[8,512]{1,0:T(8,128)S(1)}, /*index=5*/s32[]{:T(128)}, s32[]{:T(128)}) while((s32[]{:T(128)}, f32[512,128]{1,0:T(8,128)S(1)}, s32[8,512]{1,0:T(8,128)S(1)}, s32[8,512]{1,0:T(8,128)S(1)}, ...), condition=%wide.region_18.18_spmd.clone, body=%wide.region_17.17_spmd.clone.sunk | while | flops 403177472 | bytes 542815 | solution.py:73
  278.5 2.1 multiply_reduce_fusion.5
  280.6 39.3 %all-reduce.8 = (f32[]{:T(128)}, f32[]{:T(128)}) all-reduce(f32[]{:T(128)} %get-tuple-element.792, f32[]{:T(128)} %get-tuple-element.793), channel_id=1, replica_groups=mesh['gx'=8,'gy'=4] {'gx','gy'}, use_global_device_ids=true, to_apply=%region_13.13 | all-reduce | flops 2 | bytes 16 | tf_op jit(solution)/shard_map/while/body/eval_jaxpr/psum | solution.py:160
  325.0 4.8 collective-permute-start.1
  329.9 7.2 %while.73 = (s32[]{:T(128)}, f32[8,512]{1,0:T(8,128)S(1)}, s32[8,512]{1,0:T(8,128)S(1)}, s32[8,512]{1,0:T(8,128)S(1)}, f32[512,128]{1,0:T(8,128)S(1)}, /*index=5*/s32[]{:T(128)}, s32[]{:T(128)}) while((s32[]{:T(128)}, f32[8,512]{1,0:T(8,128)S(1)}, s32[8,512]{1,0:T(8,128)S(1)}, s32[8,512]{1,0:T(8,128)S(1)}, f32[512,128]{1,0:T(8,128)S(1)}, ...), condition=%wide.region_16.16_spmd, body=%wide.region_14.15_spmd.sunk | while | flops 403111424 | bytes 280661 | solution.py:55
  337.7 6.0 all-to-all-start
  344.4 5.9 all-to-all-done
  351.2 5.7 fusion.112
  358.5 3.3 all-to-all-start.1
  364.5 3.9 all-to-all-done.1
  368.3 10.5 %while.74 = (s32[]{:T(128)}, f32[512,128]{1,0:T(8,128)S(1)}, s32[8,512]{1,0:T(8,128)S(1)}, s32[8,512]{1,0:T(8,128)S(1)}, f32[8,512]{1,0:T(8,128)S(1)}, /*index=5*/s32[]{:T(128)}, s32[]{:T(128)}) while((s32[]{:T(128)}, f32[512,128]{1,0:T(8,128)S(1)}, s32[8,512]{1,0:T(8,128)S(1)}, s32[8,512]{1,0:T(8,128)S(1)}, ...), condition=%wide.region_18.18_spmd.clone, body=%wide.region_17.17_spmd.clone.sunk | while | flops 403177472 | bytes 542815 | solution.py:73
  379.6 2.1 multiply_reduce_fusion.5
  381.7 39.3 %all-reduce.8 = (f32[]{:T(128)}, f32[]{:T(128)}) all-reduce(f32[]{:T(128)} %get-tuple-element.792, f32[]{:T(128)} %get-tuple-element.793), channel_id=1, replica_groups=mesh['gx'=8,'gy'=4] {'gx','gy'}, use_global_device_ids=true, to_apply=%region_13.13 | all-reduce | flops 2 | bytes 16 | tf_op jit(solution)/shard_map/while/body/eval_jaxpr/psum | solution.py:160
  426.1 4.8 collective-permute-start.1
  430.9 7.2 %while.73 = (s32[]{:T(128)}, f32[8,512]{1,0:T(8,128)S(1)}, s32[8,512]{1,0:T(8,128)S(1)}, s32[8,512]{1,0:T(8,128)S(1)}, f32[512,128]{1,0:T(8,128)S(1)}, /*index=5*/s32[]{:T(128)}, s32[]{:T(128)}) while((s32[]{:T(128)}, f32[8,512]{1,0:T(8,128)S(1)}, s32[8,512]{1,0:T(8,128)S(1)}, s32[8,512]{1,0:T(8,128)S(1)}, f32[512,128]{1,0:T(8,128)S(1)}, ...), condition=%wide.region_16.16_spmd, body=%wide.region_14.15_spmd.sunk | while | flops 403111424 | bytes 280661 | solution.py:55
  438.7 6.0 all-to-all-start
  445.4 5.9 all-to-all-done
  452.2 5.7 fusion.112
  459.5 3.3 all-to-all-start.1
  465.5 3.9 all-to-all-done.1
  469.4 10.5 %while.74 = (s32[]{:T(128)}, f32[512,128]{1,0:T(8,128)S(1)}, s32[8,512]{1,0:T(8,128)S(1)}, s32[8,512]{1,0:T(8,128)S(1)}, f32[8,512]{1,0:T(8,128)S(1)}, /*index=5*/s32[]{:T(128)}, s32[]{:T(128)}) while((s32[]{:T(128)}, f32[512,128]{1,0:T(8,128)S(1)}, s32[8,512]{1,0:T(8,128)S(1)}, s32[8,512]{1,0:T(8,128)S(1)}, ...), condition=%wide.region_18.18_spmd.clone, body=%wide.region_17.17_spmd.clone.sunk | while | flops 403177472 | bytes 542815 | solution.py:73
  480.6 2.1 multiply_reduce_fusion.5
  482.7 39.3 %all-reduce.8 = (f32[]{:T(128)}, f32[]{:T(128)}) all-reduce(f32[]{:T(128)} %get-tuple-element.792, f32[]{:T(128)} %get-tuple-element.793), channel_id=1, replica_groups=mesh['gx'=8,'gy'=4] {'gx','gy'}, use_global_device_ids=true, to_apply=%region_13.13 | all-reduce | flops 2 | bytes 16 | tf_op jit(solution)/shard_map/while/body/eval_jaxpr/psum | solution.py:160
  527.1 4.8 collective-permute-start.1
  531.9 7.2 %while.73 = (s32[]{:T(128)}, f32[8,512]{1,0:T(8,128)S(1)}, s32[8,512]{1,0:T(8,128)S(1)}, s32[8,512]{1,0:T(8,128)S(1)}, f32[512,128]{1,0:T(8,128)S(1)}, /*index=5*/s32[]{:T(128)}, s32[]{:T(128)}) while((s32[]{:T(128)}, f32[8,512]{1,0:T(8,128)S(1)}, s32[8,512]{1,0:T(8,128)S(1)}, s32[8,512]{1,0:T(8,128)S(1)}, f32[512,128]{1,0:T(8,128)S(1)}, ...), condition=%wide.region_16.16_spmd, body=%wide.region_14.15_spmd.sunk | while | flops 403111424 | bytes 280661 | solution.py:55
  539.8 6.0 all-to-all-start
  546.4 5.9 all-to-all-done
  553.2 5.7 fusion.112
  560.5 3.3 all-to-all-start.1
  566.5 3.9 all-to-all-done.1
  570.4 10.5 %while.74 = (s32[]{:T(128)}, f32[512,128]{1,0:T(8,128)S(1)}, s32[8,512]{1,0:T(8,128)S(1)}, s32[8,512]{1,0:T(8,128)S(1)}, f32[8,512]{1,0:T(8,128)S(1)}, /*index=5*/s32[]{:T(128)}, s32[]{:T(128)}) while((s32[]{:T(128)}, f32[512,128]{1,0:T(8,128)S(1)}, s32[8,512]{1,0:T(8,128)S(1)}, s32[8,512]{1,0:T(8,128)S(1)}, ...), condition=%wide.region_18.18_spmd.clone, body=%wide.region_17.17_spmd.clone.sunk | while | flops 403177472 | bytes 542815 | solution.py:73
  581.6 2.1 multiply_reduce_fusion.5
  583.7 39.3 %all-reduce.8 = (f32[]{:T(128)}, f32[]{:T(128)}) all-reduce(f32[]{:T(128)} %get-tuple-element.792, f32[]{:T(128)} %get-tuple-element.793), channel_id=1, replica_groups=mesh['gx'=8,'gy'=4] {'gx','gy'}, use_global_device_ids=true, to_apply=%region_13.13 | all-reduce | flops 2 | bytes 16 | tf_op jit(solution)/shard_map/while/body/eval_jaxpr/psum | solution.py:160
  (443 shorter events, 168.9 us)
Async XLA Ops:
  4.4 12.7 %collective-permute-start.4 = (f32[1,32,128]{2,1,0:T(8,128)S(1)}, f32[1,32,128]{2,1,0:T(8,128)S(1)}, u32[]{:S(2)}, u32[]{:S(2)}) collective-permute-start(f32[1,32,128]{2,1,0:T(8,128)S(1)} %get-tuple-element.465), channel_id=1, source_target_pairs={{0,4},{4,8},{8,12},{12,16},{16,20},{20,24},{24,28},{1,5},{5,9},{9,... | collective-permute-start | bytes 49160 | tf_op jit(solution)/shard_map/ppermute | solution.py:13
  9.3 7.8 %collective-permute-start.5 = (f32[16,1,128]{2,1,0:T(1,128)S(1)}, f32[16,1,128]{2,1,0:T(1,128)S(1)}, u32[]{:S(2)}, u32[]{:S(2)}) collective-permute-start(f32[16,1,128]{2,1,0:T(1,128)S(1)} %broadcast_select_fusion), channel_id=1, source_target_pairs={{0,1},{1,2},{2,3},{4,5},{5,6},{6,7},{8,9},{9,10},{10,11},{12,13},{... | collective-permute-start | bytes 24584 | tf_op jit(solution)/shard_map/ppermute | solution.py:13
  17.1 31.2 %copy-start.2 = (s32[16,256]{1,0:T(8,128)S(1)}, s32[16,256]{1,0:T(8,128)}, u32[]{:S(2)}) copy-start(s32[16,256]{1,0:T(8,128)} %param.31) | copy-start | bytes 49156
  19.2 11.5 %all-to-all-start.2 = ((s32[8,2,256]{2,1,0:T(2,128)}), s32[8,2,256]{2,1,0:T(2,128)S(1)}, u32[]{:S(2)}, u32[]{:S(2)}) async-start(s32[8,2,256]{2,1,0:T(2,128)} %reshape.150), calls=%async_computation.2 | async-start | bytes 32768 | tf_op jit(solution)/shard_map/all_to_all | solution.py:112
  38.5 9.8 %all-to-all-start.3 = ((f32[8,2,256]{2,1,0:T(2,128)}), f32[8,2,256]{2,1,0:T(2,128)S(1)}, u32[]{:S(2)}, u32[]{:S(2)}) async-start(f32[8,2,256]{2,1,0:T(2,128)} %copy.14), calls=%async_computation.3 | async-start | bytes 32768 | tf_op jit(solution)/shard_map/all_to_all | solution.py:124
  41.8 19.8 %collective-permute-start.6 = (f32[1,32,128]{2,1,0:T(8,128)S(1)}, f32[1,32,128]{2,1,0:T(8,128)S(1)}, u32[]{:S(2)}, u32[]{:S(2)}) collective-permute-start(f32[1,32,128]{2,1,0:T(8,128)S(1)} %get-tuple-element.488), channel_id=1, source_target_pairs={{4,0},{8,4},{12,8},{16,12},{20,16},{24,20},{28,24},{5,1},{9,5},{13... | collective-permute-start | bytes 49160 | tf_op jit(solution)/shard_map/ppermute | solution.py:24
  43.1 18.5 %collective-permute-start.7 = (f32[1,32,128]{2,1,0:T(8,128)S(1)}, f32[1,32,128]{2,1,0:T(8,128)S(1)}, u32[]{:S(2)}, u32[]{:S(2)}) collective-permute-start(f32[1,32,128]{2,1,0:T(8,128)S(1)} %get-tuple-element.487), channel_id=1, source_target_pairs={{0,4},{4,8},{8,12},{12,16},{16,20},{20,24},{24,28},{1,5},{5,9},{9,... | collective-permute-start | bytes 49160 | tf_op jit(solution)/shard_map/ppermute | solution.py:23
  49.1 29.6 %copy-start = (f32[16,32,128]{2,1,0:T(8,128)S(1)}, f32[16,32,128]{2,1,0:T(8,128)}, u32[]{:S(2)}) copy-start(f32[16,32,128]{2,1,0:T(8,128)} %param.26) | copy-start | bytes 786436
  56.3 11.8 %all-to-all-start.4 = ((f32[8,2,256]{2,1,0:T(2,128)}), f32[8,2,256]{2,1,0:T(2,128)S(1)}, u32[]{:S(2)}, u32[]{:S(2)}) async-start(f32[8,2,256]{2,1,0:T(2,128)} %reshape.155), calls=%async_computation.4 | async-start | bytes 32768 | tf_op jit(solution)/shard_map/all_to_all | solution.py:136
  61.6 17.1 %collective-permute-start.8 = (f32[18,1,128]{2,1,0:T(1,128)S(1)}, f32[18,1,128]{2,1,0:T(1,128)S(1)}, u32[]{:S(2)}, u32[]{:S(2)}) collective-permute-start(f32[18,1,128]{2,1,0:T(1,128)S(1)} %get-tuple-element.483), channel_id=1, source_target_pairs={{1,0},{2,1},{3,2},{5,4},{6,5},{7,6},{9,8},{10,9},{11,10},{13,12},{... | collective-permute-start | bytes 27656 | tf_op jit(solution)/shard_map/ppermute | solution.py:24
  62.9 15.8 %collective-permute-start.9 = (f32[18,1,128]{2,1,0:T(1,128)S(1)}, f32[18,1,128]{2,1,0:T(1,128)S(1)}, u32[]{:S(2)}, u32[]{:S(2)}) collective-permute-start(f32[18,1,128]{2,1,0:T(1,128)S(1)} %get-tuple-element.484), channel_id=1, source_target_pairs={{0,1},{1,2},{2,3},{4,5},{5,6},{6,7},{8,9},{9,10},{10,11},{12,13},{... | collective-permute-start | bytes 27656 | tf_op jit(solution)/shard_map/ppermute | solution.py:23
  121.7 38.0 %collective-permute-start = (f32[1,32,128]{2,1,0:T(8,128)S(1)}, f32[1,32,128]{2,1,0:T(8,128)S(1)}, u32[]{:S(2)}, u32[]{:S(2)}) collective-permute-start(f32[1,32,128]{2,1,0:T(8,128)S(1)} %get-tuple-element.788), channel_id=1, source_target_pairs={{4,0},{8,4},{12,8},{16,12},{20,16},{24,20},{28,24},{5,1},{9,5},{13... | collective-permute-start | bytes 49160 | tf_op jit(solution)/shard_map/while/body/eval_jaxpr/ppermute | solution.py:24
  123.0 36.7 %collective-permute-start.1 = (f32[1,32,128]{2,1,0:T(8,128)S(1)}, f32[1,32,128]{2,1,0:T(8,128)S(1)}, u32[]{:S(2)}, u32[]{:S(2)}) collective-permute-start(f32[1,32,128]{2,1,0:T(8,128)S(1)} %get-tuple-element.789), channel_id=1, source_target_pairs={{0,4},{4,8},{8,12},{12,16},{16,20},{20,24},{24,28},{1,5},{5,9},{9,... | collective-permute-start | bytes 49160 | tf_op jit(solution)/shard_map/while/body/eval_jaxpr/ppermute | solution.py:23
  135.6 12.6 %all-to-all-start = ((f32[8,2,256]{2,1,0:T(2,128)}), f32[8,2,256]{2,1,0:T(2,128)S(1)}, u32[]{:S(2)}, u32[]{:S(2)}) async-start(f32[8,2,256]{2,1,0:T(2,128)} %copy.40), calls=%async_computation | async-start | bytes 32768 | tf_op jit(solution)/shard_map/while/body/eval_jaxpr/all_to_all | solution.py:124
  156.4 9.8 %all-to-all-start.1 = ((f32[8,2,256]{2,1,0:T(2,128)}), f32[8,2,256]{2,1,0:T(2,128)S(1)}, u32[]{:S(2)}, u32[]{:S(2)}) async-start(f32[8,2,256]{2,1,0:T(2,128)} %reshape.181), calls=%async_computation.1 | async-start | bytes 32768 | tf_op jit(solution)/shard_map/while/body/eval_jaxpr/all_to_all | solution.py:136
  159.8 17.0 %collective-permute-start.2 = (f32[18,1,128]{2,1,0:T(1,128)S(1)}, f32[18,1,128]{2,1,0:T(1,128)S(1)}, u32[]{:S(2)}, u32[]{:S(2)}) collective-permute-start(f32[18,1,128]{2,1,0:T(1,128)S(1)} %get-tuple-element.790), channel_id=1, source_target_pairs={{0,1},{1,2},{2,3},{4,5},{5,6},{6,7},{8,9},{9,10},{10,11},{12,13},{... | collective-permute-start | bytes 27656 | tf_op jit(solution)/shard_map/while/body/eval_jaxpr/ppermute | solution.py:23
  161.1 15.7 %collective-permute-start.3 = (f32[18,1,128]{2,1,0:T(1,128)S(1)}, f32[18,1,128]{2,1,0:T(1,128)S(1)}, u32[]{:S(2)}, u32[]{:S(2)}) collective-permute-start(f32[18,1,128]{2,1,0:T(1,128)S(1)} %get-tuple-element.791), channel_id=1, source_target_pairs={{1,0},{2,1},{3,2},{5,4},{6,5},{7,6},{9,8},{10,9},{11,10},{13,12},{... | collective-permute-start | bytes 27656 | tf_op jit(solution)/shard_map/while/body/eval_jaxpr/ppermute | solution.py:24
  176.8 0.7 copy-start.1
  222.7 38.1 %collective-permute-start = (f32[1,32,128]{2,1,0:T(8,128)S(1)}, f32[1,32,128]{2,1,0:T(8,128)S(1)}, u32[]{:S(2)}, u32[]{:S(2)}) collective-permute-start(f32[1,32,128]{2,1,0:T(8,128)S(1)} %get-tuple-element.788), channel_id=1, source_target_pairs={{4,0},{8,4},{12,8},{16,12},{20,16},{24,20},{28,24},{5,1},{9,5},{13... | collective-permute-start | bytes 49160 | tf_op jit(solution)/shard_map/while/body/eval_jaxpr/ppermute | solution.py:24
  224.0 36.8 %collective-permute-start.1 = (f32[1,32,128]{2,1,0:T(8,128)S(1)}, f32[1,32,128]{2,1,0:T(8,128)S(1)}, u32[]{:S(2)}, u32[]{:S(2)}) collective-permute-start(f32[1,32,128]{2,1,0:T(8,128)S(1)} %get-tuple-element.789), channel_id=1, source_target_pairs={{0,4},{4,8},{8,12},{12,16},{16,20},{20,24},{24,28},{1,5},{5,9},{9,... | collective-permute-start | bytes 49160 | tf_op jit(solution)/shard_map/while/body/eval_jaxpr/ppermute | solution.py:23
  236.7 12.5 %all-to-all-start = ((f32[8,2,256]{2,1,0:T(2,128)}), f32[8,2,256]{2,1,0:T(2,128)S(1)}, u32[]{:S(2)}, u32[]{:S(2)}) async-start(f32[8,2,256]{2,1,0:T(2,128)} %copy.40), calls=%async_computation | async-start | bytes 32768 | tf_op jit(solution)/shard_map/while/body/eval_jaxpr/all_to_all | solution.py:124
  257.4 9.8 %all-to-all-start.1 = ((f32[8,2,256]{2,1,0:T(2,128)}), f32[8,2,256]{2,1,0:T(2,128)S(1)}, u32[]{:S(2)}, u32[]{:S(2)}) async-start(f32[8,2,256]{2,1,0:T(2,128)} %reshape.181), calls=%async_computation.1 | async-start | bytes 32768 | tf_op jit(solution)/shard_map/while/body/eval_jaxpr/all_to_all | solution.py:136
  260.8 17.0 %collective-permute-start.2 = (f32[18,1,128]{2,1,0:T(1,128)S(1)}, f32[18,1,128]{2,1,0:T(1,128)S(1)}, u32[]{:S(2)}, u32[]{:S(2)}) collective-permute-start(f32[18,1,128]{2,1,0:T(1,128)S(1)} %get-tuple-element.790), channel_id=1, source_target_pairs={{0,1},{1,2},{2,3},{4,5},{5,6},{6,7},{8,9},{9,10},{10,11},{12,13},{... | collective-permute-start | bytes 27656 | tf_op jit(solution)/shard_map/while/body/eval_jaxpr/ppermute | solution.py:23
  262.1 15.7 %collective-permute-start.3 = (f32[18,1,128]{2,1,0:T(1,128)S(1)}, f32[18,1,128]{2,1,0:T(1,128)S(1)}, u32[]{:S(2)}, u32[]{:S(2)}) collective-permute-start(f32[18,1,128]{2,1,0:T(1,128)S(1)} %get-tuple-element.791), channel_id=1, source_target_pairs={{1,0},{2,1},{3,2},{5,4},{6,5},{7,6},{9,8},{10,9},{11,10},{13,12},{... | collective-permute-start | bytes 27656 | tf_op jit(solution)/shard_map/while/body/eval_jaxpr/ppermute | solution.py:24
  277.8 0.7 copy-start.1
  323.7 38.1 %collective-permute-start = (f32[1,32,128]{2,1,0:T(8,128)S(1)}, f32[1,32,128]{2,1,0:T(8,128)S(1)}, u32[]{:S(2)}, u32[]{:S(2)}) collective-permute-start(f32[1,32,128]{2,1,0:T(8,128)S(1)} %get-tuple-element.788), channel_id=1, source_target_pairs={{4,0},{8,4},{12,8},{16,12},{20,16},{24,20},{28,24},{5,1},{9,5},{13... | collective-permute-start | bytes 49160 | tf_op jit(solution)/shard_map/while/body/eval_jaxpr/ppermute | solution.py:24
  325.0 36.8 %collective-permute-start.1 = (f32[1,32,128]{2,1,0:T(8,128)S(1)}, f32[1,32,128]{2,1,0:T(8,128)S(1)}, u32[]{:S(2)}, u32[]{:S(2)}) collective-permute-start(f32[1,32,128]{2,1,0:T(8,128)S(1)} %get-tuple-element.789), channel_id=1, source_target_pairs={{0,4},{4,8},{8,12},{12,16},{16,20},{20,24},{24,28},{1,5},{5,9},{9,... | collective-permute-start | bytes 49160 | tf_op jit(solution)/shard_map/while/body/eval_jaxpr/ppermute | solution.py:23
  337.7 12.5 %all-to-all-start = ((f32[8,2,256]{2,1,0:T(2,128)}), f32[8,2,256]{2,1,0:T(2,128)S(1)}, u32[]{:S(2)}, u32[]{:S(2)}) async-start(f32[8,2,256]{2,1,0:T(2,128)} %copy.40), calls=%async_computation | async-start | bytes 32768 | tf_op jit(solution)/shard_map/while/body/eval_jaxpr/all_to_all | solution.py:124
  358.5 9.8 %all-to-all-start.1 = ((f32[8,2,256]{2,1,0:T(2,128)}), f32[8,2,256]{2,1,0:T(2,128)S(1)}, u32[]{:S(2)}, u32[]{:S(2)}) async-start(f32[8,2,256]{2,1,0:T(2,128)} %reshape.181), calls=%async_computation.1 | async-start | bytes 32768 | tf_op jit(solution)/shard_map/while/body/eval_jaxpr/all_to_all | solution.py:136
  361.9 17.0 %collective-permute-start.2 = (f32[18,1,128]{2,1,0:T(1,128)S(1)}, f32[18,1,128]{2,1,0:T(1,128)S(1)}, u32[]{:S(2)}, u32[]{:S(2)}) collective-permute-start(f32[18,1,128]{2,1,0:T(1,128)S(1)} %get-tuple-element.790), channel_id=1, source_target_pairs={{0,1},{1,2},{2,3},{4,5},{5,6},{6,7},{8,9},{9,10},{10,11},{12,13},{... | collective-permute-start | bytes 27656 | tf_op jit(solution)/shard_map/while/body/eval_jaxpr/ppermute | solution.py:23
  363.2 15.7 %collective-permute-start.3 = (f32[18,1,128]{2,1,0:T(1,128)S(1)}, f32[18,1,128]{2,1,0:T(1,128)S(1)}, u32[]{:S(2)}, u32[]{:S(2)}) collective-permute-start(f32[18,1,128]{2,1,0:T(1,128)S(1)} %get-tuple-element.791), channel_id=1, source_target_pairs={{1,0},{2,1},{3,2},{5,4},{6,5},{7,6},{9,8},{10,9},{11,10},{13,12},{... | collective-permute-start | bytes 27656 | tf_op jit(solution)/shard_map/while/body/eval_jaxpr/ppermute | solution.py:24
  378.9 0.7 copy-start.1
  424.8 38.1 %collective-permute-start = (f32[1,32,128]{2,1,0:T(8,128)S(1)}, f32[1,32,128]{2,1,0:T(8,128)S(1)}, u32[]{:S(2)}, u32[]{:S(2)}) collective-permute-start(f32[1,32,128]{2,1,0:T(8,128)S(1)} %get-tuple-element.788), channel_id=1, source_target_pairs={{4,0},{8,4},{12,8},{16,12},{20,16},{24,20},{28,24},{5,1},{9,5},{13... | collective-permute-start | bytes 49160 | tf_op jit(solution)/shard_map/while/body/eval_jaxpr/ppermute | solution.py:24
  426.1 36.8 %collective-permute-start.1 = (f32[1,32,128]{2,1,0:T(8,128)S(1)}, f32[1,32,128]{2,1,0:T(8,128)S(1)}, u32[]{:S(2)}, u32[]{:S(2)}) collective-permute-start(f32[1,32,128]{2,1,0:T(8,128)S(1)} %get-tuple-element.789), channel_id=1, source_target_pairs={{0,4},{4,8},{8,12},{12,16},{16,20},{20,24},{24,28},{1,5},{5,9},{9,... | collective-permute-start | bytes 49160 | tf_op jit(solution)/shard_map/while/body/eval_jaxpr/ppermute | solution.py:23
  438.7 12.5 %all-to-all-start = ((f32[8,2,256]{2,1,0:T(2,128)}), f32[8,2,256]{2,1,0:T(2,128)S(1)}, u32[]{:S(2)}, u32[]{:S(2)}) async-start(f32[8,2,256]{2,1,0:T(2,128)} %copy.40), calls=%async_computation | async-start | bytes 32768 | tf_op jit(solution)/shard_map/while/body/eval_jaxpr/all_to_all | solution.py:124
  459.5 9.8 %all-to-all-start.1 = ((f32[8,2,256]{2,1,0:T(2,128)}), f32[8,2,256]{2,1,0:T(2,128)S(1)}, u32[]{:S(2)}, u32[]{:S(2)}) async-start(f32[8,2,256]{2,1,0:T(2,128)} %reshape.181), calls=%async_computation.1 | async-start | bytes 32768 | tf_op jit(solution)/shard_map/while/body/eval_jaxpr/all_to_all | solution.py:136
  462.9 17.0 %collective-permute-start.2 = (f32[18,1,128]{2,1,0:T(1,128)S(1)}, f32[18,1,128]{2,1,0:T(1,128)S(1)}, u32[]{:S(2)}, u32[]{:S(2)}) collective-permute-start(f32[18,1,128]{2,1,0:T(1,128)S(1)} %get-tuple-element.790), channel_id=1, source_target_pairs={{0,1},{1,2},{2,3},{4,5},{5,6},{6,7},{8,9},{9,10},{10,11},{12,13},{... | collective-permute-start | bytes 27656 | tf_op jit(solution)/shard_map/while/body/eval_jaxpr/ppermute | solution.py:23
  464.2 15.7 %collective-permute-start.3 = (f32[18,1,128]{2,1,0:T(1,128)S(1)}, f32[18,1,128]{2,1,0:T(1,128)S(1)}, u32[]{:S(2)}, u32[]{:S(2)}) collective-permute-start(f32[18,1,128]{2,1,0:T(1,128)S(1)} %get-tuple-element.791), channel_id=1, source_target_pairs={{1,0},{2,1},{3,2},{5,4},{6,5},{7,6},{9,8},{10,9},{11,10},{13,12},{... | collective-permute-start | bytes 27656 | tf_op jit(solution)/shard_map/while/body/eval_jaxpr/ppermute | solution.py:24
  479.9 0.7 copy-start.1
  525.8 38.1 %collective-permute-start = (f32[1,32,128]{2,1,0:T(8,128)S(1)}, f32[1,32,128]{2,1,0:T(8,128)S(1)}, u32[]{:S(2)}, u32[]{:S(2)}) collective-permute-start(f32[1,32,128]{2,1,0:T(8,128)S(1)} %get-tuple-element.788), channel_id=1, source_target_pairs={{4,0},{8,4},{12,8},{16,12},{20,16},{24,20},{28,24},{5,1},{9,5},{13... | collective-permute-start | bytes 49160 | tf_op jit(solution)/shard_map/while/body/eval_jaxpr/ppermute | solution.py:24
  527.1 36.8 %collective-permute-start.1 = (f32[1,32,128]{2,1,0:T(8,128)S(1)}, f32[1,32,128]{2,1,0:T(8,128)S(1)}, u32[]{:S(2)}, u32[]{:S(2)}) collective-permute-start(f32[1,32,128]{2,1,0:T(8,128)S(1)} %get-tuple-element.789), channel_id=1, source_target_pairs={{0,4},{4,8},{8,12},{12,16},{16,20},{20,24},{24,28},{1,5},{5,9},{9,... | collective-permute-start | bytes 49160 | tf_op jit(solution)/shard_map/while/body/eval_jaxpr/ppermute | solution.py:23
  539.8 12.5 %all-to-all-start = ((f32[8,2,256]{2,1,0:T(2,128)}), f32[8,2,256]{2,1,0:T(2,128)S(1)}, u32[]{:S(2)}, u32[]{:S(2)}) async-start(f32[8,2,256]{2,1,0:T(2,128)} %copy.40), calls=%async_computation | async-start | bytes 32768 | tf_op jit(solution)/shard_map/while/body/eval_jaxpr/all_to_all | solution.py:124
  560.5 9.8 %all-to-all-start.1 = ((f32[8,2,256]{2,1,0:T(2,128)}), f32[8,2,256]{2,1,0:T(2,128)S(1)}, u32[]{:S(2)}, u32[]{:S(2)}) async-start(f32[8,2,256]{2,1,0:T(2,128)} %reshape.181), calls=%async_computation.1 | async-start | bytes 32768 | tf_op jit(solution)/shard_map/while/body/eval_jaxpr/all_to_all | solution.py:136
  563.9 17.0 %collective-permute-start.2 = (f32[18,1,128]{2,1,0:T(1,128)S(1)}, f32[18,1,128]{2,1,0:T(1,128)S(1)}, u32[]{:S(2)}, u32[]{:S(2)}) collective-permute-start(f32[18,1,128]{2,1,0:T(1,128)S(1)} %get-tuple-element.790), channel_id=1, source_target_pairs={{0,1},{1,2},{2,3},{4,5},{5,6},{6,7},{8,9},{9,10},{10,11},{12,13},{... | collective-permute-start | bytes 27656 | tf_op jit(solution)/shard_map/while/body/eval_jaxpr/ppermute | solution.py:23
  565.2 15.7 %collective-permute-start.3 = (f32[18,1,128]{2,1,0:T(1,128)S(1)}, f32[18,1,128]{2,1,0:T(1,128)S(1)}, u32[]{:S(2)}, u32[]{:S(2)}) collective-permute-start(f32[18,1,128]{2,1,0:T(1,128)S(1)} %get-tuple-element.791), channel_id=1, source_target_pairs={{1,0},{2,1},{3,2},{5,4},{6,5},{7,6},{9,8},{10,9},{11,10},{13,12},{... | collective-permute-start | bytes 27656 | tf_op jit(solution)/shard_map/while/body/eval_jaxpr/ppermute | solution.py:24
  580.9 0.7 copy-start.1
where the time goes:
time: 631 us; the launch traced here: 627 us
  blocking collectives  236 us (37%)
  matrix products  144 us (23%)
  starting transfers between devices  120 us (19%)
  waiting for transfers between devices  58 us (9%)
  other arithmetic  24.8 us (4%)
  local copies, waits for them, and re-layouts  22.7 us (4%)
  loops' own time  19.4 us (3%)
    psum x6, blocking collectives, paired(): lax.psum((jnp.sum(residual * precon), jnp.sum(precon * applied)), ('gx',...  236 us
    dot_general x48, matrix products, add_block(): lax.dot_general(column_table(triple[0], columns), spread_rows, (((0,), (0...  60.3 us
    dot_general x48, matrix products, pick_block(): jnp.dot(column_table(pair[0], columns), field_cols, precision=lax.Precisi...  38.2 us
    ppermute x12, starting transfers between devices, with_halo(): before = lax.ppermute(last, axis, up)  38.1 us
    dot_general x6, matrix products, well_term(): jnp.einsum('wij,wj->wi', schur_blocks, gathered, precision=lax.Precision....  34 us
    all_to_all x6, starting transfers between devices, well_term(): lax.all_to_all(picked, 'gx', split_axis=0, concat_axis=0, tiled=True)  33.2 us
    all_to_all x6, waiting for transfers between devices, well_term(): lax.all_to_all(picked, 'gx', split_axis=0, concat_axis=0, tiled=True)  29.9 us
    all_to_all x6, starting transfers between devices, well_term(): lax.all_to_all(outgoing, 'gx', split_axis=0, concat_axis=0, tiled=True)  21.9 us
  transfers between devices with their start and end apart: 39, of which 13 were waited for; matrix products, arithmetic and copies ran while one was open for 25% of the time, Pallas kernels for 0%

commit v1 on v0

v1 whole, which is shorter than its diff:
```python
import functools

import jax
import jax.numpy as jnp
from jax import lax
from jax.experimental import pallas as pl
from jax.experimental.pallas import tpu as pltpu
from jax.sharding import PartitionSpec as P

WCAP = 2
ITERS = 6
ROWS = 4
MESH = pl.DeviceIdType.MESH


def split_bf16(values):
    high = values.astype(jnp.bfloat16).astype(jnp.float32)
    return high, values - high


def kernel(
    n,
    ny,
    rows_x,
    rows_y,
    region_ref,
    rhs_ref,
    acc_ref,
    tx_ref,
    ty_ref,
    tz_ref,
    cells_ref,
    live_ref,
    schur_hbm,
    x_ref,
    r_ref,
    schur_vm,
    schur_two,
    onehot,
    vl_ref,
    lay_ref,
    live_slot,
    req_send,
    req_recv,
    send_b,
    recv_b,
    send_c,
    recv_c,
    send_g,
    recv_g,
    ysend,
    xrecv,
    yrecv,
    yface_send,
    xface_recv,
    yface_recv,
    fx_ref,
    fy_ref,
    py_ref,
    fz_ref,
    pz_ref,
    inv_ref,
    m_ref,
    w_ref,
    z_ref,
    p_ref,
    s_ref,
    nloc_ref,
    dots_ref,
    local_sem,
    req_ss,
    req_rs,
    face_ss,
    face_rs,
    halo_ss,
    halo_rs,
    b_ss,
    b_rs,
    c_ss,
    c_rs,
    g_ss,
    g_rs,
):
    cols, layers = rhs_ref.shape
    wells, perf = cells_ref.shape
    chunk = WCAP * perf
    shift = layers.bit_length() - 1
    assert layers == 1 << shift
    me, my = lax.axis_index("gx"), lax.axis_index("gy")

    def at_x(d):
        return {"gx": lax.rem(me + (d + n), n)}

    def at_y(d):
        return {"gy": lax.rem(my + (d + ny), ny)}

    def remote(src, dst, ss, rs, where):
        return pltpu.make_async_remote_copy(
            src_ref=src, dst_ref=dst, send_sem=ss, recv_sem=rs, device_id=where, device_id_type=MESH
        )

    schur_copy = pltpu.make_async_copy(schur_hbm, schur_vm, local_sem)
    schur_copy.start()
    barrier = pltpu.get_barrier_semaphore()
    for d in range(1, n):
        pl.semaphore_signal(barrier, inc=1, device_id=at_x(d), device_id_type=MESH)
    for d in range(1, ny):
        pl.semaphore_signal(barrier, inc=1, device_id=at_y(d), device_id_type=MESH)

    well_at = []
    for d in range(n):
        peer = lax.rem(me + d, n)
        found = [jnp.int32(0)] * WCAP
        count = jnp.int32(0)
        for w in range(wells):
            match = region_ref[w, 0] == peer
            for j in range(WCAP):
                found[j] = jnp.where(jnp.logical_and(match, count == j), jnp.int32(w), found[j])
            count = count + match.astype(jnp.int32)
        well_at.append(found)
        for j in range(WCAP):
            used = (count > j).astype(jnp.int32)
            cells = cells_ref[pl.ds(found[j], 1), :] * used
            live = live_ref[pl.ds(found[j], 1), :] * used
            target = req_send if d else req_recv
            target[d, j : j + 1, :] = cells
            live_slot[d, j : j + 1, :] = live.astype(jnp.float32)
    yface_send[...] = ty_ref[pl.ds(rows_y - 1, rows_x, stride=rows_y), :]

    pl.semaphore_wait(barrier, n - 1 + ny - 1)
    req_out = [
        remote(req_send.at[d], req_recv.at[n - d], req_ss.at[d], req_rs.at[n - d], at_x(d))
        for d in range(1, n)
    ]
    req_in = [
        remote(req_send.at[d], req_recv.at[d], req_ss.at[d], req_rs.at[d], at_x(d)) for d in range(1, n)
    ]
    face_out = [
        remote(
            tx_ref.at[pl.ds(cols - rows_y, rows_y)], xface_recv, face_ss.at[0], face_rs.at[0], at_x(1)
        ),
        remote(yface_send, yface_recv, face_ss.at[1], face_rs.at[1], at_y(1)),
    ]
    for copy in req_out + face_out:
        copy.start()

    last_x = me == n - 1
    last_y = my == ny - 1
    lane = lax.broadcasted_iota(jnp.int32, (rows_y, layers), 1)
    row = lax.broadcasted_iota(jnp.int32, (rows_y, layers), 0)
    zeros = jnp.zeros((rows_y, layers), jnp.float32)
    for copy in face_out:
        copy.wait()
    fx_ref[0:rows_y, :] = jnp.where(me == 0, 0.0, xface_recv[...])
    gamma = jnp.zeros((8, layers), jnp.float32)
    for i in range(rows_x):
        at = slice(i * rows_y, (i + 1) * rows_y)
        after = slice((i + 1) * rows_y, (i + 2) * rows_y)
        fx = tx_ref[at, :]
        if i == rows_x - 1:
            fx = jnp.where(last_x, 0.0, fx)
        fx_ref[after, :] = fx
        fy = ty_ref[at, :]
        below = jnp.where(my == 0, 0.0, yface_recv[i : i + 1, :])
        py = jnp.where(row == 0, below, pltpu.roll(fy, 1, 0))
        fy = jnp.where(jnp.logical_and(last_y, row == rows_y - 1), 0.0, fy)
        fy_ref[at, :] = fy
        py_ref[at, :] = py
        fz = jnp.where(lane == layers - 1, 0.0, tz_ref[at, :])
        pz = pltpu.roll(fz, 1, 1)
        fz_ref[at, :] = fz
        pz_ref[at, :] = pz
        diagonal = acc_ref[at, :] + fx + fx_ref[at, :] + fy + py + fz + pz
        inverse = 1.0 / diagonal
        inv_ref[at, :] = inverse
        r = rhs_ref[at, :]
        r_ref[at, :] = r
        u = r * inverse
        m_ref[at, :] = u
        for ref in (x_ref, w_ref, z_ref, p_ref, s_ref):
            ref[at, :] = zeros
    dots_ref[...] = jnp.zeros_like(dots_ref)

    column = lax.broadcasted_iota(jnp.int32, (cols, chunk), 0)
    for d in range(n):
        if d:
            req_in[d - 1].wait_recv()
        cells = jnp.concatenate([req_recv[d, j : j + 1, :] for j in range(WCAP)], 1)
        lay_ref[d] = jnp.bitwise_and(cells, layers - 1)
        onehot[:, d * chunk : (d + 1) * chunk] = (
            (column == lax.shift_right_logical(cells, shift)).astype(jnp.float32).astype(jnp.bfloat16)
        )
    for copy in req_out:
        copy.wait_send()

    schur_copy.wait()
    for d in range(n):
        for j in range(WCAP):
            slot = d * WCAP + j
            block = schur_vm[well_at[d][j]]
            high = block.astype(jnp.bfloat16)
            schur_two[slot, 0:perf, :] = high
            schur_two[slot, perf : 2 * perf, :] = (block - high.astype(jnp.float32)).astype(jnp.bfloat16)

    layer = lax.broadcasted_iota(jnp.int32, (layers, chunk), 0)
    pick_row = lax.broadcasted_iota(jnp.int32, (16, perf), 0)

    def b_copy(par, d, slot):
        return remote(send_b.at[par, d], recv_b.at[par, slot], b_ss.at[par, d], b_rs.at[par, slot], at_x(d))

    def c_copy(par, d, slot):
        return remote(send_c.at[par, d], recv_c.at[par, slot], c_ss.at[par, d], c_rs.at[par, slot], at_x(d))

    def g_copy(par, d, slot):
        return remote(send_g.at[par], recv_g.at[par, slot], g_ss.at[par, d], g_rs.at[par, slot], at_y(d))

    def halo_copies(par):
        return [
            remote(
                m_ref.at[pl.ds(cols - rows_y, rows_y)],
                xrecv.at[par, 0],
                halo_ss.at[par, 0],
                halo_rs.at[par, 0],
                at_x(1),
            ),
            remote(
                m_ref.at[pl.ds(0, rows_y)], xrecv.at[par, 1], halo_ss.at[par, 1], halo_rs.at[par, 1], at_x(-1)
            ),
            remote(ysend.at[par, 0], yrecv.at[par, 0], halo_ss.at[par, 2], halo_rs.at[par, 2], at_y(1)),
            remote(ysend.at[par, 1], yrecv.at[par, 1], halo_ss.at[par, 3], halo_rs.at[par, 3], at_y(-1)),
        ]

    def start_sums(par):
        total = recv_b[par, 0, 2:3, :]
        for d in range(1, n):
            total = total + recv_b[par, d, 2:3, :]
        send_g[par] = total
        for d in range(1, ny):
            g_copy(par, d, ny - d).start()
        return total

    def end_sums(par, total):
        for d in range(1, ny):
            g_copy(par, d, d).wait_recv()
            total = total + recv_g[par, d]
        for d in range(1, ny):
            g_copy(par, d, d).wait_send()
        gam = jnp.sum(total[:, :layers], axis=1, keepdims=True)
        dlt = jnp.sum(total[:, layers:], axis=1, keepdims=True)
        return jnp.broadcast_to(gam, (1, layers)), jnp.broadcast_to(dlt, (1, layers))

    def step(k, carried):
        gam_old, a_old = carried
        par = lax.rem(k, 2)
        ysend[par, 0] = m_ref[pl.ds(rows_y - 1, rows_x, stride=rows_y), :]
        ysend[par, 1] = m_ref[pl.ds(0, rows_x, stride=rows_y), :]
        halos = halo_copies(par)
        for copy in halos:
            copy.start()

        turned = m_ref[...].T
        high, low = split_bf16(turned)
        lhs = jnp.concatenate([high, low], 0).astype(jnp.bfloat16)
        dots = dots_ref[...]
        for d in list(range(1, n)) + [0]:
            part = jnp.dot(
                lhs, onehot[:, d * chunk : (d + 1) * chunk], preferred_element_type=jnp.float32
            )
            part = part[:layers] + part[layers:]
            picked = jnp.sum(jnp.where(layer == lay_ref[d], part, 0.0), axis=0, keepdims=True)
            target = send_b if d else recv_b
            for j in range(WCAP):
                target[par, d, j : j + 1, :] = picked[:, j * perf : (j + 1) * perf]
            target[par, d, 2:3, :] = dots
            if d:
                b_copy(par, d, n - d).start()

        for copy in halos:
            copy.wait()
        for i in range(rows_x):
            at = slice(i * rows_y, (i + 1) * rows_y)
            after = slice((i + 1) * rows_y, (i + 2) * rows_y)
            m = m_ref[at, :]
            below = m_ref[(i - 1) * rows_y : i * rows_y, :] if i else xrecv[par, 0]
            above = m_ref[after, :] if i < rows_x - 1 else xrecv[par, 1]
            y_prev = jnp.where(row == 0, yrecv[par, 0, i : i + 1, :], pltpu.roll(m, 1, 0))
            y_next = jnp.where(row == rows_y - 1, yrecv[par, 1, i : i + 1, :], pltpu.roll(m, rows_y - 1, 0))
            nloc_ref[at, :] = (
                acc_ref[at, :] * m
                + fx_ref[after, :] * (m - above)
                + fx_ref[at, :] * (m - below)
                + fy_ref[at, :] * (m - y_next)
                + py_ref[at, :] * (m - y_prev)
                + fz_ref[at, :] * (m - pltpu.roll(m, layers - 1, 1))
                + pz_ref[at, :] * (m - pltpu.roll(m, 1, 1))
            )

        for d in range(n):
            if d:
                b_copy(par, d, d).wait_recv()
            target = send_c if d else recv_c
            for j in range(WCAP):
                live = live_slot[d, j : j + 1, :]
                high, low = split_bf16(recv_b[par, d, j : j + 1, :] * live)
                left = jnp.where(pick_row == 0, high, jnp.where(pick_row == 1, low, 0.0)).astype(jnp.bfloat16)
                pushed = jnp.dot(
                    jnp.concatenate([left, left], 1),
                    schur_two[d * WCAP + j],
                    preferred_element_type=jnp.float32,
                )
                target[par, d, j : j + 1, :] = jnp.sum(pushed, axis=0, keepdims=True) * live
            if d:
                c_copy(par, d, n - d).start()
        total = start_sums(par)
        gam, dlt = end_sums(par, total)
        b = jnp.where(k <= 1, 0.0, gam / gam_old)
        a = jnp.where(k == 0, 0.0, jnp.where(k == 1, gam / dlt, gam / (dlt - b * gam / a_old)))
        a_w = jnp.where(k == 0, -1.0, a)
        gamma = jnp.zeros((8, layers), jnp.float32)
        for i in range(rows_x):
            at = slice(i * rows_y, (i + 1) * rows_y)
            inverse = inv_ref[at, :]
            r = r_ref[at, :]
            p = r * inverse + b * p_ref[at, :]
            s = w_ref[at, :] + b * s_ref[at, :]
            p_ref[at, :] = p
            s_ref[at, :] = s
            x_ref[at, :] = x_ref[at, :] + a * p
            r = r - a * s
            r_ref[at, :] = r
            gamma = gamma + jnp.sum((r * r * inverse).reshape(rows_y // 8, 8, layers), axis=0)

        for d in range(n):
            if d:
                c_copy(par, d, d).wait_recv()
            back = jnp.concatenate([recv_c[par, d, j : j + 1, :] for j in range(WCAP)], 1)
            high, low = split_bf16(back)
            here = layer == lay_ref[d]
            span = slice(d * chunk, (d + 1) * chunk)
            vl_ref[0:layers, span] = jnp.where(here, high, 0.0).astype(jnp.bfloat16)
            vl_ref[layers : 2 * layers, span] = jnp.where(here, low, 0.0).astype(jnp.bfloat16)
        wide = lax.dot_general(
            onehot[...], vl_ref[...], (((1,), (1,)), ((), ())), preferred_element_type=jnp.float32
        )
        spread = wide[:, :layers] + wide[:, layers:]
        delta = jnp.zeros((8, layers), jnp.float32)
        for i in range(rows_x):
            at = slice(i * rows_y, (i + 1) * rows_y)
            z = nloc_ref[at, :] + spread[at, :] + b * z_ref[at, :]
            z_ref[at, :] = z
            w = w_ref[at, :] - a_w * z
            w_ref[at, :] = w
            m = w * inv_ref[at, :]
            m_ref[at, :] = m
            delta = delta + jnp.sum((m * r_ref[at, :]).reshape(rows_y // 8, 8, layers), axis=0)
        dots_ref[:, :layers] = jnp.sum(gamma, axis=0, keepdims=True)
        dots_ref[:, layers:] = jnp.sum(delta, axis=0, keepdims=True)
        for d in range(1, n):
            b_copy(par, d, d).wait_send()
            c_copy(par, d, d).wait_send()
        return gam, a

    ones = jnp.ones((1, layers), jnp.float32)
    gam_old, a_old = lax.fori_loop(0, ITERS, step, (ones, ones))

    par = ITERS % 2
    recv_b[par, 0, 2:3, :] = dots_ref[...]
    for d in range(1, n):
        send_b[par, d, 2:3, :] = dots_ref[...]
        b_copy(par, d, n - d).start()
    for d in range(1, n):
        b_copy(par, d, d).wait_recv()
    total = start_sums(par)
    for d in range(1, n):
        b_copy(par, d, d).wait_send()
    gam, dlt = end_sums(par, total)
    b = gam / gam_old
    a = gam / (dlt - b * gam / a_old)
    for i in range(rows_x):
        at = slice(i * rows_y, (i + 1) * rows_y)
        r = r_ref[at, :]
        p = r * inv_ref[at, :] + b * p_ref[at, :]
        s = w_ref[at, :] + b * s_ref[at, :]
        x_ref[at, :] = x_ref[at, :] + a * p
        r_ref[at, :] = r - a * s


def local(
    right_side,
    accumulation,
    trans_x,
    trans_y,
    trans_z,
    perf_cells,
    perf_live,
    well_region,
    schur_blocks,
):
    rows_x, rows_y, layers = right_side.shape
    cols = rows_x * rows_y
    wells, perf = perf_cells.shape
    n, ny = lax.axis_size("gx"), lax.axis_size("gy")
    chunk = WCAP * perf
    f32, bf16, i32 = jnp.float32, jnp.bfloat16, jnp.int32
    vmem, dma = pltpu.VMEM, pltpu.SemaphoreType.DMA
    field = vmem((cols, layers), f32)
    fields = [value.reshape(cols, layers) for value in (right_side, accumulation, trans_x, trans_y, trans_z)]
    in_vmem = pl.BlockSpec(memory_space=pltpu.VMEM)
    outs = pl.pallas_call(
        functools.partial(kernel, n, ny, rows_x, rows_y),
        out_shape=[jax.ShapeDtypeStruct((cols, layers), f32)] * 2,
        in_specs=[pl.BlockSpec(memory_space=pltpu.SMEM)]
        + [in_vmem] * 7
        + [pl.BlockSpec(memory_space=pl.ANY)],
        out_specs=[in_vmem] * 2,
        scratch_shapes=[
            vmem((wells, perf, perf), f32),
            vmem((n * WCAP, 2 * perf, perf), bf16),
            vmem((cols, n * chunk), bf16),
            vmem((2 * layers, n * chunk), bf16),
            vmem((n, 1, chunk), i32),
            vmem((n, WCAP, perf), f32),
            vmem((n, WCAP, perf), i32),
            vmem((n, WCAP, perf), i32),
            vmem((2, n, ROWS, 2 * layers), f32),
            vmem((2, n, ROWS, 2 * layers), f32),
            vmem((2, n, WCAP, perf), f32),
            vmem((2, n, WCAP, perf), f32),
            vmem((2, 1, 2 * layers), f32),
            vmem((2, ny, 1, 2 * layers), f32),
            vmem((2, 2, rows_x, layers), f32),
            vmem((2, 2, rows_y, layers), f32),
            vmem((2, 2, rows_x, layers), f32),
            vmem((rows_x, layers), f32),
            vmem((rows_y, layers), f32),
            vmem((rows_x, layers), f32),
            vmem((cols + rows_y, layers), f32),
        ]
        + [field] * 11
        + [
            vmem((1, 2 * layers), f32),
            dma,
            dma((n,)),
            dma((n,)),
            dma((2,)),
            dma((2,)),
            dma((2, 4)),
            dma((2, 4)),
            dma((2, n)),
            dma((2, n)),
            dma((2, n)),
            dma((2, n)),
            dma((2, ny)),
            dma((2, ny)),
        ],
        compiler_params=pltpu.CompilerParams(
            collective_id=0, has_side_effects=True, vmem_limit_bytes=60 * 1024 * 1024
        ),
    )(well_region, *fields, perf_cells, perf_live, schur_blocks)
    return tuple(value.reshape(right_side.shape) for value in outs)


def solution(mesh):
    field, rows = P("gx", "gy", None), P(("gx", "gy"), None)
    return jax.shard_map(
        local,
        mesh=mesh,
        in_specs=(field,) * 5 + (rows,) * 3 + (P(("gx", "gy"), None, None),),
        out_specs=(field, field),
        check_vma=False,
    )
```

time: 631 us -> 97.2 us (0.15)
  blocking collectives: 236 us -> 0 us
  matrix products: 144 us -> 0 us
  starting transfers between devices: 120 us -> 0 us
  Pallas kernels: 0 us -> 91.6 us
  waiting for transfers between devices: 58 us -> 0 us
  other arithmetic: 24.8 us -> 0 us
  loops' own time: 19.4 us -> 0 us
  local copies, waits for them, and re-layouts: 22.7 us -> 4.67 us
    psum x6 -> x0, blocking collectives: 236 us -> none  [paired(): lax.psum((jnp.sum(residual * precon), jnp.sum(precon * applied)), ('gx',...]
    dot_general x114 -> x0, matrix products: 144 us -> none  [the longest x48 60.3 us: add_block(): lax.dot_general(column_table(triple[0], columns), spread_rows, (((0,), (0...]
    pallas_call x0 -> x1, Pallas kernels: none -> 91.6 us  [local(): pl.pallas_call(functools.partial(kernel, n, ny, rows_x, rows_y), out_shap...]
    all_to_all x13 -> x0, starting transfers between devices: 59.9 us -> none  [the longest x6 33.2 us: well_term(): lax.all_to_all(picked, 'gx', split_axis=0, concat_axis=0, tiled=True)]
    ppermute x26 -> x0, starting transfers between devices: 59.9 us -> none  [the longest x12 38.1 us: with_halo(): before = lax.ppermute(last, axis, up)]
    all_to_all x13 -> x0, waiting for transfers between devices: 57.9 us -> none  [the longest x6 29.9 us: well_term(): lax.all_to_all(picked, 'gx', split_axis=0, concat_axis=0, tiled=True)]
    another operation x13 -> x0, loops' own time: 19.4 us -> none  [the longest x1 15.9 us: local(): lax.fori_loop(0, ITERS - 1, iterate, (solution, residual, precon, applied...]
    reduce_sum x7 -> x0, other arithmetic: 12.5 us -> none  [the longest x6 11.6 us: paired(): jnp.sum(precon * applied)]
  transfers between devices with their start and end apart: 39 -> 0, of which waited for: 13 -> 0; matrix products, arithmetic and copies ran while one was open for 25% -> 0% of each run, Pallas kernels for 0% -> 0%
where the time goes in v1:
time: 97.2 us; the launch traced here: 97 us
  Pallas kernels  91.6 us (94%)
  local copies, waits for them, and re-layouts  4.67 us (5%)
    pallas_call x1, Pallas kernels, local(): pl.pallas_call(functools.partial(kernel, n, ny, rows_x, rows_y), out_shap...  91.6 us
    unnamed x3, local copies, waits for them, and re-layouts  4.67 us

profile of v1, /device:TPU:0, one launch (start us, length us, event | category | flops | bytes accessed | tf_op | source)
XLA Modules:
  0.0 97.0 jit_solution(2011128547898351976)
XLA Ops:
  0.6 1.3 %copy.11.region_ref = s32[16,1]{1,0:T(8,128)} copy(s32[16,1]{0,1:T(1,128)} %param.16) | data formatting | bytes 128 | tf_op args[7]
  2.0 91.6 %shard_map.104 = (f32[512,128]{1,0:T(8,128)}, f32[512,128]{1,0:T(8,128)}) custom-call(s32[16,1]{1,0:T(8,128)} %copy.11.region_ref, f32[512,128]{1,0:T(8,128)} %bitcast.9, f32[512,128]{1,0:T(8,128)} %bitcast.10, f32[512,128]{1,0:T(8,128)} %bitcast.11, f32[512,128]{1,0:T(8,128)} %bitcast.12, f32[512,128]{1,0:T(8,128)} %bitcast.13, s32[16,256]{1,0:T(8,128)} %cells_ref.1, ...), custom_call_target="tpu_custom_call" | custom-call | tf_op jit(solution)/shard_map/pallas_call | solution.py:409
  93.6 1.7 %copy.14 = f32[16,32,128]{2,1,0:T(8,128)} copy(f32[16,32,128]{2,1,0:T(8,128)} %bitcast.8) | data formatting | bytes 524288
  95.3 1.7 %copy.15 = f32[16,32,128]{2,1,0:T(8,128)} copy(f32[16,32,128]{2,1,0:T(8,128)} %bitcast.7) | data formatting | bytes 524288

commit v2 on v1

--- a/solution.py
+++ b/solution.py
@@ -9,7 +9,8 @@
 
 WCAP = 2
 ITERS = 6
-ROWS = 4
+GROUPS = (6, 8)
+EARLY = 6
 MESH = pl.DeviceIdType.MESH
 
 
@@ -24,16 +25,21 @@
     rows_x,
     rows_y,
     region_ref,
+    rhs_hbm,
+    acc_hbm,
+    tx_hbm,
+    ty_hbm,
+    tz_hbm,
+    cells_ref,
+    live_ref,
+    schur_hbm,
+    x_ref,
+    r_ref,
     rhs_ref,
     acc_ref,
     tx_ref,
     ty_ref,
     tz_ref,
-    cells_ref,
-    live_ref,
-    schur_hbm,
-    x_ref,
-    r_ref,
     schur_vm,
     schur_two,
     onehot,
@@ -68,6 +74,7 @@
     nloc_ref,
     dots_ref,
     local_sem,
+    field_sem,
     req_ss,
     req_rs,
     face_ss,
@@ -85,8 +92,18 @@
     wells, perf = cells_ref.shape
     chunk = WCAP * perf
     shift = layers.bit_length() - 1
-    assert layers == 1 << shift
+    assert layers == 1 << shift and n == 1 << (n.bit_length() - 1)
     me, my = lax.axis_index("gx"), lax.axis_index("gy")
+
+    def across(d):
+        peer = me
+        for bit in range(n.bit_length() - 1):
+            if d >> bit & 1:
+                peer = peer + (1 << bit) * (1 - 2 * lax.rem(lax.div(me, 1 << bit), 2))
+        return peer
+
+    def at_peer(d):
+        return {"gx": across(d)}
 
     def at_x(d):
         return {"gx": lax.rem(me + (d + n), n)}
@@ -100,40 +117,52 @@
         )
 
     schur_copy = pltpu.make_async_copy(schur_hbm, schur_vm, local_sem)
+    loads = [
+        pltpu.make_async_copy(src, dst, field_sem.at[i])
+        for i, (src, dst) in enumerate(
+            (
+                (ty_hbm, ty_ref),
+                (tx_hbm, tx_ref),
+                (tz_hbm, tz_ref),
+                (acc_hbm, acc_ref),
+                (rhs_hbm, rhs_ref),
+            )
+        )
+    ]
+    for copy in loads:
+        copy.start()
     schur_copy.start()
+    xrecv[...] = jnp.zeros_like(xrecv)
     barrier = pltpu.get_barrier_semaphore()
     for d in range(1, n):
-        pl.semaphore_signal(barrier, inc=1, device_id=at_x(d), device_id_type=MESH)
+        pl.semaphore_signal(barrier, inc=1, device_id=at_peer(d), device_id_type=MESH)
     for d in range(1, ny):
         pl.semaphore_signal(barrier, inc=1, device_id=at_y(d), device_id_type=MESH)
 
     well_at = []
     for d in range(n):
-        peer = lax.rem(me + d, n)
+        peer = across(d)
         found = [jnp.int32(0)] * WCAP
         count = jnp.int32(0)
         for w in range(wells):
-            match = region_ref[w, 0] == peer
+            match = region_ref[0, w] == peer
             for j in range(WCAP):
                 found[j] = jnp.where(jnp.logical_and(match, count == j), jnp.int32(w), found[j])
             count = count + match.astype(jnp.int32)
         well_at.append(found)
+        target = req_send if d else req_recv
         for j in range(WCAP):
             used = (count > j).astype(jnp.int32)
-            cells = cells_ref[pl.ds(found[j], 1), :] * used
-            live = live_ref[pl.ds(found[j], 1), :] * used
-            target = req_send if d else req_recv
-            target[d, j : j + 1, :] = cells
-            live_slot[d, j : j + 1, :] = live.astype(jnp.float32)
+            span = slice(j * perf, (j + 1) * perf)
+            target[d, :, span] = cells_ref[pl.ds(found[j], 1), :] * used
+            live_slot[d, :, span] = (live_ref[pl.ds(found[j], 1), :] * used).astype(jnp.float32)
+    loads[0].wait()
+    loads[1].wait()
     yface_send[...] = ty_ref[pl.ds(rows_y - 1, rows_x, stride=rows_y), :]
 
     pl.semaphore_wait(barrier, n - 1 + ny - 1)
-    req_out = [
-        remote(req_send.at[d], req_recv.at[n - d], req_ss.at[d], req_rs.at[n - d], at_x(d))
-        for d in range(1, n)
-    ]
-    req_in = [
-        remote(req_send.at[d], req_recv.at[d], req_ss.at[d], req_rs.at[d], at_x(d)) for d in range(1, n)
+    requests = [
+        remote(req_send.at[d], req_recv.at[d], req_ss.at[d], req_rs.at[d], at_peer(d)) for d in range(1, n)
     ]
     face_out = [
         remote(
@@ -141,18 +170,28 @@
         ),
         remote(yface_send, yface_recv, face_ss.at[1], face_rs.at[1], at_y(1)),
     ]
-    for copy in req_out + face_out:
+    for copy in requests[::-1] + face_out:
         copy.start()
+
+    schur_copy.wait()
+    for d in range(n):
+        for j in range(WCAP):
+            slot = d * WCAP + j
+            block = schur_vm[well_at[d][j]]
+            high = block.astype(jnp.bfloat16)
+            schur_two[slot, 0:perf, :] = high
+            schur_two[slot, perf : 2 * perf, :] = (block - high.astype(jnp.float32)).astype(jnp.bfloat16)
 
     last_x = me == n - 1
     last_y = my == ny - 1
     lane = lax.broadcasted_iota(jnp.int32, (rows_y, layers), 1)
     row = lax.broadcasted_iota(jnp.int32, (rows_y, layers), 0)
     zeros = jnp.zeros((rows_y, layers), jnp.float32)
+    for copy in loads[2:]:
+        copy.wait()
     for copy in face_out:
         copy.wait()
     fx_ref[0:rows_y, :] = jnp.where(me == 0, 0.0, xface_recv[...])
-    gamma = jnp.zeros((8, layers), jnp.float32)
     for i in range(rows_x):
         at = slice(i * rows_y, (i + 1) * rows_y)
         after = slice((i + 1) * rows_y, (i + 2) * rows_y)
@@ -184,32 +223,26 @@
     column = lax.broadcasted_iota(jnp.int32, (cols, chunk), 0)
     for d in range(n):
         if d:
-            req_in[d - 1].wait_recv()
-        cells = jnp.concatenate([req_recv[d, j : j + 1, :] for j in range(WCAP)], 1)
+            requests[d - 1].wait_recv()
+        cells = req_recv[d]
         lay_ref[d] = jnp.bitwise_and(cells, layers - 1)
         onehot[:, d * chunk : (d + 1) * chunk] = (
             (column == lax.shift_right_logical(cells, shift)).astype(jnp.float32).astype(jnp.bfloat16)
         )
-    for copy in req_out:
+    for copy in requests:
         copy.wait_send()
-
-    schur_copy.wait()
-    for d in range(n):
-        for j in range(WCAP):
-            slot = d * WCAP + j
-            block = schur_vm[well_at[d][j]]
-            high = block.astype(jnp.bfloat16)
-            schur_two[slot, 0:perf, :] = high
-            schur_two[slot, perf : 2 * perf, :] = (block - high.astype(jnp.float32)).astype(jnp.bfloat16)
 
     layer = lax.broadcasted_iota(jnp.int32, (layers, chunk), 0)
     pick_row = lax.broadcasted_iota(jnp.int32, (16, perf), 0)
 
-    def b_copy(par, d, slot):
-        return remote(send_b.at[par, d], recv_b.at[par, slot], b_ss.at[par, d], b_rs.at[par, slot], at_x(d))
-
-    def c_copy(par, d, slot):
-        return remote(send_c.at[par, d], recv_c.at[par, slot], c_ss.at[par, d], c_rs.at[par, slot], at_x(d))
+    half = layers // 2
+    first_half = lax.broadcasted_iota(jnp.int32, (1, layers), 1) < half
+
+    def b_copy(par, d):
+        return remote(send_b.at[par, d], recv_b.at[par, d], b_ss.at[par, d], b_rs.at[par, d], at_peer(d))
+
+    def c_copy(par, d):
+        return remote(send_c.at[par, d], recv_c.at[par, d], c_ss.at[par, d], c_rs.at[par, d], at_peer(d))
 
     def g_copy(par, d, slot):
         return remote(send_g.at[par], recv_g.at[par, slot], g_ss.at[par, d], g_rs.at[par, slot], at_y(d))
@@ -231,9 +264,9 @@
         ]
 
     def start_sums(par):
-        total = recv_b[par, 0, 2:3, :]
+        total = recv_b[par, 0, :, chunk:]
         for d in range(1, n):
-            total = total + recv_b[par, d, 2:3, :]
+            total = total + recv_b[par, d, :, chunk:]
         send_g[par] = total
         for d in range(1, ny):
             g_copy(par, d, ny - d).start()
@@ -245,8 +278,8 @@
             total = total + recv_g[par, d]
         for d in range(1, ny):
             g_copy(par, d, d).wait_send()
-        gam = jnp.sum(total[:, :layers], axis=1, keepdims=True)
-        dlt = jnp.sum(total[:, layers:], axis=1, keepdims=True)
+        gam = jnp.sum(jnp.where(first_half, total, 0.0), axis=1, keepdims=True)
+        dlt = jnp.sum(jnp.where(first_half, 0.0, total), axis=1, keepdims=True)
         return jnp.broadcast_to(gam, (1, layers)), jnp.broadcast_to(dlt, (1, layers))
 
     def step(k, carried):
@@ -255,27 +288,59 @@
         ysend[par, 0] = m_ref[pl.ds(rows_y - 1, rows_x, stride=rows_y), :]
         ysend[par, 1] = m_ref[pl.ds(0, rows_x, stride=rows_y), :]
         halos = halo_copies(par)
-        for copy in halos:
+        x_up, x_down = halos[:2]
+        pl.when(me < n - 1)(x_up.start)
+        pl.when(me > 0)(x_down.start)
+        for copy in halos[2:]:
             copy.start()
 
         turned = m_ref[...].T
         high, low = split_bf16(turned)
         lhs = jnp.concatenate([high, low], 0).astype(jnp.bfloat16)
         dots = dots_ref[...]
-        for d in list(range(1, n)) + [0]:
+        for d in range(n - 1, -1, -1):
             part = jnp.dot(
                 lhs, onehot[:, d * chunk : (d + 1) * chunk], preferred_element_type=jnp.float32
             )
             part = part[:layers] + part[layers:]
             picked = jnp.sum(jnp.where(layer == lay_ref[d], part, 0.0), axis=0, keepdims=True)
             target = send_b if d else recv_b
+            target[par, d, :, :chunk] = picked
+            target[par, d, :, chunk:] = dots
+            if d:
+                b_copy(par, d).start()
+
+        def push(d):
+            if d:
+                b_copy(par, d).wait_recv()
+            target = send_c if d else recv_c
             for j in range(WCAP):
-                target[par, d, j : j + 1, :] = picked[:, j * perf : (j + 1) * perf]
-            target[par, d, 2:3, :] = dots
+                span = slice(j * perf, (j + 1) * perf)
+                live = live_slot[d, :, span]
+                high, low = split_bf16(recv_b[par, d, :, span] * live)
+                left = jnp.where(pick_row == 0, high, jnp.where(pick_row == 1, low, 0.0)).astype(jnp.bfloat16)
+                pushed = jnp.dot(
+                    jnp.concatenate([left, left], 1),
+                    schur_two[d * WCAP + j],
+                    preferred_element_type=jnp.float32,
+                )
+                target[par, d, :, span] = jnp.sum(pushed, axis=0, keepdims=True) * live
             if d:
-                b_copy(par, d, n - d).start()
-
-        for copy in halos:
+                c_copy(par, d).start()
+
+        for d in range(EARLY):
+            push(d)
+        @pl.when(me < n - 1)
+        def _():
+            x_up.wait_send()
+            x_down.wait_recv()
+
+        @pl.when(me > 0)
+        def _():
+            x_up.wait_recv()
+            x_down.wait_send()
+
+        for copy in halos[2:]:
             copy.wait()
         for i in range(rows_x):
             at = slice(i * rows_y, (i + 1) * rows_y)
@@ -294,23 +359,8 @@
                 + fz_ref[at, :] * (m - pltpu.roll(m, layers - 1, 1))
                 + pz_ref[at, :] * (m - pltpu.roll(m, 1, 1))
             )
-
-        for d in range(n):
-            if d:
-                b_copy(par, d, d).wait_recv()
-            target = send_c if d else recv_c
-            for j in range(WCAP):
-                live = live_slot[d, j : j + 1, :]
-                high, low = split_bf16(recv_b[par, d, j : j + 1, :] * live)
-                left = jnp.where(pick_row == 0, high, jnp.where(pick_row == 1, low, 0.0)).astype(jnp.bfloat16)
-                pushed = jnp.dot(
-                    jnp.concatenate([left, left], 1),
-                    schur_two[d * WCAP + j],
-                    preferred_element_type=jnp.float32,
-                )
-                target[par, d, j : j + 1, :] = jnp.sum(pushed, axis=0, keepdims=True) * live
-            if d:
-                c_copy(par, d, n - d).start()
+        for d in range(EARLY, n):
+            push(d)
         total = start_sums(par)
         gam, dlt = end_sums(par, total)
         b = jnp.where(k <= 1, 0.0, gam / gam_old)
@@ -330,49 +380,58 @@
             r_ref[at, :] = r
             gamma = gamma + jnp.sum((r * r * inverse).reshape(rows_y // 8, 8, layers), axis=0)
 
-        for d in range(n):
-            if d:
-                c_copy(par, d, d).wait_recv()
-            back = jnp.concatenate([recv_c[par, d, j : j + 1, :] for j in range(WCAP)], 1)
-            high, low = split_bf16(back)
-            here = layer == lay_ref[d]
-            span = slice(d * chunk, (d + 1) * chunk)
-            vl_ref[0:layers, span] = jnp.where(here, high, 0.0).astype(jnp.bfloat16)
-            vl_ref[layers : 2 * layers, span] = jnp.where(here, low, 0.0).astype(jnp.bfloat16)
-        wide = lax.dot_general(
-            onehot[...], vl_ref[...], (((1,), (1,)), ((), ())), preferred_element_type=jnp.float32
-        )
-        spread = wide[:, :layers] + wide[:, layers:]
+        ends = [n * part // 8 for part in GROUPS]
+        for first, end in zip([0] + ends[:-1], ends):
+            for d in range(first, end):
+                if d:
+                    c_copy(par, d).wait_recv()
+                high, low = split_bf16(recv_c[par, d])
+                here = layer == lay_ref[d]
+                span = slice(d * chunk, (d + 1) * chunk)
+                vl_ref[0:layers, span] = jnp.where(here, high, 0.0).astype(jnp.bfloat16)
+                vl_ref[layers : 2 * layers, span] = jnp.where(here, low, 0.0).astype(jnp.bfloat16)
+            span = slice(first * chunk, end * chunk)
+            wide = lax.dot_general(
+                onehot[:, span],
+                vl_ref[:, span],
+                (((1,), (1,)), ((), ())),
+                preferred_element_type=jnp.float32,
+            )
+            if end < n:
+                nloc_ref[...] += wide[:, :layers] + wide[:, layers:]
         delta = jnp.zeros((8, layers), jnp.float32)
         for i in range(rows_x):
             at = slice(i * rows_y, (i + 1) * rows_y)
-            z = nloc_ref[at, :] + spread[at, :] + b * z_ref[at, :]
+            z = nloc_ref[at, :] + (wide[at, :layers] + wide[at, layers:]) + b * z_ref[at, :]
             z_ref[at, :] = z
             w = w_ref[at, :] - a_w * z
             w_ref[at, :] = w
             m = w * inv_ref[at, :]
             m_ref[at, :] = m
             delta = delta + jnp.sum((m * r_ref[at, :]).reshape(rows_y // 8, 8, layers), axis=0)
-        dots_ref[:, :layers] = jnp.sum(gamma, axis=0, keepdims=True)
-        dots_ref[:, layers:] = jnp.sum(delta, axis=0, keepdims=True)
+        gamma = jnp.sum(gamma, axis=0, keepdims=True)
+        delta = jnp.sum(delta, axis=0, keepdims=True)
+        dots_ref[...] = jnp.where(
+            first_half, gamma + pltpu.roll(gamma, half, 1), delta + pltpu.roll(delta, half, 1)
+        )
         for d in range(1, n):
-            b_copy(par, d, d).wait_send()
-            c_copy(par, d, d).wait_send()
+            b_copy(par, d).wait_send()
+            c_copy(par, d).wait_send()
         return gam, a
 
     ones = jnp.ones((1, layers), jnp.float32)
     gam_old, a_old = lax.fori_loop(0, ITERS, step, (ones, ones))
 
     par = ITERS % 2
-    recv_b[par, 0, 2:3, :] = dots_ref[...]
+    recv_b[par, 0, :, chunk:] = dots_ref[...]
+    for d in range(n - 1, 0, -1):
+        send_b[par, d, :, chunk:] = dots_ref[...]
+        b_copy(par, d).start()
     for d in range(1, n):
-        send_b[par, d, 2:3, :] = dots_ref[...]
-        b_copy(par, d, n - d).start()
-    for d in range(1, n):
-        b_copy(par, d, d).wait_recv()
+        b_copy(par, d).wait_recv()
     total = start_sums(par)
     for d in range(1, n):
-        b_copy(par, d, d).wait_send()
+        b_copy(par, d).wait_send()
     gam, dlt = end_sums(par, total)
     b = gam / gam_old
     a = gam / (dlt - b * gam / a_old)
@@ -383,6 +442,11 @@
         s = w_ref[at, :] + b * s_ref[at, :]
         x_ref[at, :] = x_ref[at, :] + a * p
         r_ref[at, :] = r - a * s
+
+
+def hand_on(x_ref, r_ref, x_out, r_out):
+    x_out[...] = x_ref[...]
+    r_out[...] = r_ref[...]
 
 
 def local(
@@ -410,24 +474,26 @@
         functools.partial(kernel, n, ny, rows_x, rows_y),
         out_shape=[jax.ShapeDtypeStruct((cols, layers), f32)] * 2,
         in_specs=[pl.BlockSpec(memory_space=pltpu.SMEM)]
-        + [in_vmem] * 7
+        + [pl.BlockSpec(memory_space=pl.ANY)] * 5
+        + [in_vmem] * 2
         + [pl.BlockSpec(memory_space=pl.ANY)],
         out_specs=[in_vmem] * 2,
-        scratch_shapes=[
+        scratch_shapes=[field] * 5
+        + [
             vmem((wells, perf, perf), f32),
             vmem((n * WCAP, 2 * perf, perf), bf16),
             vmem((cols, n * chunk), bf16),
             vmem((2 * layers, n * chunk), bf16),
             vmem((n, 1, chunk), i32),
-            vmem((n, WCAP, perf), f32),
-            vmem((n, WCAP, perf), i32),
-            vmem((n, WCAP, perf), i32),
-            vmem((2, n, ROWS, 2 * layers), f32),
-            vmem((2, n, ROWS, 2 * layers), f32),
-            vmem((2, n, WCAP, perf), f32),
-            vmem((2, n, WCAP, perf), f32),
-            vmem((2, 1, 2 * layers), f32),
-            vmem((2, ny, 1, 2 * layers), f32),
+            vmem((n, 1, chunk), f32),
+            vmem((n, 1, chunk), i32),
+            vmem((n, 1, chunk), i32),
+            vmem((2, n, 1, chunk + layers), f32),
+            vmem((2, n, 1, chunk + layers), f32),
+            vmem((2, n, 1, chunk), f32),
+            vmem((2, n, 1, chunk), f32),
+            vmem((2, 1, layers), f32),
+            vmem((2, ny, 1, layers), f32),
             vmem((2, 2, rows_x, layers), f32),
             vmem((2, 2, rows_y, layers), f32),
             vmem((2, 2, rows_x, layers), f32),
@@ -438,8 +504,9 @@
         ]
         + [field] * 11
         + [
-            vmem((1, 2 * layers), f32),
+            vmem((1, layers), f32),
             dma,
+            dma((5,)),
             dma((n,)),
             dma((n,)),
             dma((2,)),
@@ -456,7 +523,13 @@
         compiler_params=pltpu.CompilerParams(
             collective_id=0, has_side_effects=True, vmem_limit_bytes=60 * 1024 * 1024
         ),
-    )(well_region, *fields, perf_cells, perf_live, schur_blocks)
+    )(well_region.reshape(1, wells), *fields, perf_cells, perf_live, schur_blocks)
+    outs = pl.pallas_call(
+        hand_on,
+        out_shape=[jax.ShapeDtypeStruct((cols, layers), f32)] * 2,
+        in_specs=[in_vmem] * 2,
+        out_specs=[in_vmem] * 2,
+    )(*outs)
     return tuple(value.reshape(right_side.shape) for value in outs)
 
 

time: 97.2 us -> 92.3 us (0.950)
  local copies, waits for them, and re-layouts: 4.67 us -> 0 us
    unnamed x3 -> x0, local copies, waits for them, and re-layouts: 4.67 us -> none
    pallas_call x1, Pallas kernels: 91.6 us -> 89.6 us  [local(): pl.pallas_call(functools.partial(kernel, n, ny, rows_x, rows_y), out_shap...]
    pallas_call x0 -> x1, Pallas kernels: none -> 1.84 us  [local(): pl.pallas_call(hand_on, out_shape=[jax.ShapeDtypeStruct((cols, layers), f...]
where the time goes in v2:
time: 92.3 us; the launch traced here: 92.1 us
  Pallas kernels  91.4 us (99%)
    pallas_call x1, Pallas kernels, local(): pl.pallas_call(functools.partial(kernel, n, ny, rows_x, rows_y), out_shap...  89.6 us

profile of v2, /device:TPU:0, one launch (start us, length us, event | category | flops | bytes accessed | tf_op | source)
XLA Modules:
  0.0 92.1 jit_solution(17672296786531447436)
XLA Ops:
  0.6 89.6 %shard_map.104 = (f32[512,128]{1,0:T(8,128)}, f32[512,128]{1,0:T(8,128)}) custom-call(s32[1,16]{1,0:T(1,128)} %bitcast.13, f32[512,128]{1,0:T(8,128)} %bitcast.8, f32[512,128]{1,0:T(8,128)} %bitcast.9, f32[512,128]{1,0:T(8,128)} %bitcast.10, f32[512,128]{1,0:T(8,128)} %bitcast.11, f32[512,128]{1,0:T(8,128)} %bitcast.12, s32[16,256]{1,0:T(8,128)} %cells_ref.1, ...), custom_call_target="tpu_custom_call" | custom-call | tf_op jit(solution)/shard_map/pallas_call | solution.py:473
  90.2 1.8 %shard_map.105 = (f32[512,128]{1,0:T(8,128)}, f32[512,128]{1,0:T(8,128)}) custom-call(f32[512,128]{1,0:T(8,128)} %get-tuple-element.6.x_ref, f32[512,128]{1,0:T(8,128)} %get-tuple-element.7.r_ref), custom_call_target="tpu_custom_call" | custom-call | tf_op jit(solution)/shard_map/pallas_call | solution.py:527
